TPU v7x, 256 devices: a whole 4x4x8 slice. The times are simulated.
256 devices in a mesh: row: 16 (over x, y), col: 16 (over z, core).
Axes of the slice: x: 4, y: 4, z: 8, core: 2. Of those that a mesh axis runs over, the one named last changes fastest.
Arguments:
- trailing_slab: float32 [131072, 2048], P('row', 'col'), may hold values from -6 to 6, as said below
- panel_columns: float32 [32, 131072], P(None, 'row'), may hold values from -1870.1934 to 1870.1934
- far_image: float32 [32, 131072], P(None, 'row'), may hold values from -2048 to 2048
Outputs:
- updated_slab: float32 [131072, 2048], P('row', 'col')
- update_factor: float32 [32, 131072], P(None, 'row')
Inputs may be any that keep to these rules, and one draw needn't show every extreme that they name: Rows 0 to 2047 of trailing_slab form a symmetric block.
All inputs are finite; a program needn't handle non-finite values.
Results may differ from a plain program's by a relative error of at most 0.0003.
Values sent between devices are 32-bit elements; how exact they have to be, the bound alone decides.
A program may use at most 64 MiB of HBM per device.

v0:
```python
import jax
import jax.numpy as jnp
from jax import lax
from jax.sharding import PartitionSpec as P


def from_root(block, axis, owner):
    block = jnp.where(lax.axis_index(axis) == owner, block, jnp.zeros_like(block))
    return lax.psum(block, axis)


def product(left, right):
    return jnp.dot(left, right, precision=lax.Precision.HIGHEST, preferred_element_type=jnp.float32)


def contract(left, right, left_dim, right_dim):
    return lax.dot_general(
        left,
        right,
        (((left_dim,), (right_dim,)), ((), ())),
        precision=lax.Precision.HIGHEST,
        preferred_element_type=jnp.float32,
    )


def cholesky_rows(gram_total):
    panel_width = gram_total.shape[0]
    identity = jnp.eye(panel_width, dtype=jnp.float32)
    indices = jnp.arange(panel_width)
    lower_part = jnp.zeros((panel_width, panel_width), jnp.float32)
    for column in range(panel_width):
        onehot = identity[column]
        residue = gram_total[:, column] - product(lower_part, lower_part[column])
        pivot = jnp.sqrt(jnp.sum(residue * onehot))
        new_column = jnp.where(indices >= column, residue / pivot, 0.0)
        lower_part = lower_part + new_column[:, None] * onehot[None, :]
    return lower_part


def invert_lower(lower_part):
    panel_width = lower_part.shape[0]
    identity = jnp.eye(panel_width, dtype=jnp.float32)
    inverse = jnp.zeros((panel_width, panel_width), jnp.float32)
    for index_row in range(panel_width):
        onehot = identity[index_row]
        pivot = jnp.sum(lower_part[index_row] * onehot)
        new_row = (onehot - product(lower_part[index_row], inverse)) / pivot
        inverse = inverse + onehot[:, None] * new_row[None, :]
    return inverse


def decompose(shifted):
    panel_width = shifted.shape[0]
    identity = jnp.eye(panel_width, dtype=jnp.float32)
    indices = jnp.arange(panel_width)
    lower_unit = identity
    upper_part = shifted
    for column in range(panel_width):
        factor = jnp.where(
            indices > column, upper_part[:, column] / upper_part[column, column], 0.0
        )
        lower_unit = lower_unit + factor[:, None] * identity[column][None, :]
        upper_part = upper_part - factor[:, None] * upper_part[column][None, :]
    return (lower_unit, jnp.triu(upper_part))


def factors(gram_total, top_rows):
    panel_width = gram_total.shape[0]
    identity = jnp.eye(panel_width, dtype=jnp.float32)
    cholesky_lower = cholesky_rows(gram_total)
    cholesky_inverse = invert_lower(cholesky_lower)
    top_factor = product(cholesky_inverse, top_rows).T
    sign_flip = jnp.where(jnp.diag(top_factor) >= 0.0, -1.0, 1.0).astype(jnp.float32)
    lower_unit, upper_part = decompose(identity - top_factor * sign_flip[None, :])
    upper_inverse = invert_lower(upper_part.T).T
    root_inverse = cholesky_inverse.T
    mixing = -product(root_inverse * sign_flip[None, :], upper_inverse)
    lower_inverse = invert_lower(lower_unit)
    triangle = product(upper_part, lower_inverse.T)
    return (mixing, upper_inverse, triangle)


def local(trailing_slab, panel_columns, far_image):
    cols_dev = trailing_slab.shape[1]
    panel_width = panel_columns.shape[0]
    row_pos = lax.axis_index("row")
    col_pos = lax.axis_index("col")
    top_row = row_pos == 0
    gram_part = product(panel_columns, panel_columns.T)
    top_local = panel_columns[:, :panel_width]
    gram_total = lax.psum(gram_part, "row")
    top_rows = from_root(top_local, "row", 0)
    mixing, upper_inverse, triangle = factors(gram_total, top_rows)
    reflectors = product(mixing.T, panel_columns)
    head_rows = jnp.where(top_row, upper_inverse.T, 0.0)
    reflectors = reflectors.at[:, :panel_width].add(head_rows)
    col_start = col_pos * cols_dev
    own_reflectors = from_root(
        lax.dynamic_slice_in_dim(reflectors, col_start, cols_dev, 1), "row", 0
    )
    far_part = product(mixing.T, far_image)
    local_image = contract(own_reflectors, trailing_slab, 1, 1)
    images = lax.psum(local_image, "col") + far_part
    inner_block = lax.psum(product(reflectors, images.T), "row")
    core_block = product(product(triangle.T, inner_block), triangle)
    weights = product(triangle.T, images) - 0.5 * product(core_block.T, reflectors)
    own_weights = from_root(lax.dynamic_slice_in_dim(weights, col_start, cols_dev, 1), "row", 0)
    updated = (
        trailing_slab
        - contract(reflectors, own_weights, 0, 0)
        - contract(weights, own_reflectors, 0, 0)
    )
    return (updated, weights)


def solution(mesh):
    in_specs = (P("row", "col"), P(None, "row"), P(None, "row"))
    out_specs = (P("row", "col"), P(None, "row"))
    return jax.shard_map(local, mesh=mesh, in_specs=in_specs, out_specs=out_specs, check_vma=False)
```

profile of v0, /device:TPU:0, one launch (start us, length us, event | category | flops | bytes accessed | tf_op | source)
XLA Modules:
  0.0 674.5 jit_solution(5860183124567604668)
XLA Ops:
  9.0 2.6 fusion.969
  12.3 72.9 %all-reduce = (f32[32,32]{0,1:T(8,128)S(1)}, f32[32,32]{1,0:T(8,128)S(1)}) all-reduce(f32[32,32]{0,1:T(8,128)S(1)} %broadcast_select_fusion, f32[32,32]{1,0:T(8,128)S(1)} %fusion.969), channel_id=1, replica_groups=mesh['row'=16,'col'=16] {'row'}, use_global_device_ids=true, to_apply=%region_65.66 | all-reduce | flops 2048 | bytes 16384 | tf_op jit(solution)/shard_map/psum | solution.py:9
  166.8 0.9 fusion.131
  169.3 0.9 fusion.134
  170.2 0.9 fusion.135
  171.0 0.9 fusion.136
  171.9 0.9 fusion.137
  172.8 0.9 fusion.138
  174.5 0.9 fusion.140
  177.2 0.9 fusion.143
  178.1 0.9 fusion.144
  181.4 0.9 fusion.148
  183.2 0.9 fusion.150
  185.0 0.9 fusion.152
  190.2 0.9 fusion.158
  191.8 0.9 fusion.160
  250.8 0.9 fusion.195
  253.2 0.9 fusion.197
  254.7 0.9 fusion.198
  255.6 0.9 fusion.199
  258.0 0.9 fusion.201
  260.3 0.9 fusion.203
  261.9 0.9 fusion.204
  265.4 0.9 fusion.165
  267.0 0.9 fusion.167
  267.9 0.9 fusion.168
  268.8 0.9 fusion.169
  269.7 1.0 fusion.170
  270.7 0.9 fusion.171
  271.6 0.9 fusion.172
  274.0 0.9 fusion.206
  276.4 0.9 fusion.208
  278.8 0.9 fusion.175
  279.6 0.9 fusion.176
  282.1 0.9 fusion.178
  284.5 0.9 fusion.180
  286.0 0.9 fusion.210
  286.9 0.9 fusion.211
  287.8 0.9 fusion.212
  290.1 0.9 fusion.182
  294.1 0.9 fusion.214
  294.9 0.9 fusion.215
  295.8 0.9 fusion.216
  298.2 0.9 fusion.186
  302.1 0.9 fusion.218
  303.0 0.9 fusion.219
  303.8 0.9 fusion.220
  306.3 0.9 fusion.190
  308.5 0.9 fusion.192
  309.9 1.2 fusion.970
  312.4 69.5 %psum.44 = f32[32,128]{1,0:T(8,128)S(1)} all-reduce(f32[32,128]{1,0:T(8,128)S(1)} %dynamic-slice_select_fusion.1), channel_id=1, replica_groups=mesh['row'=16,'col'=16] {'row'}, use_global_device_ids=true, to_apply=%region_131.132 | all-reduce | flops 4096 | bytes 32768 | tf_op jit(solution)/shard_map/psum | solution.py:9
  381.9 7.4 %fusion.971 = f32[32,8192]{1,0:T(8,128)} fusion(f32[32,128]{1,0:T(8,128)S(1)} %psum.44, f32[8192,128]{1,0:T(8,128)} %param.5), kind=kOutput, calls=%fused_computation.1690 | convolution fusion | flops 402653184 | bytes 5259264 | tf_op jit(solution)/shard_map/dot_general | solution.py:17
  390.0 0.9 fusion.222
  390.9 0.9 fusion.223
  391.7 0.9 fusion.224
  392.9 105.8 %all-reduce.3.cloned.1.call-done = f32[32,8192]{1,0:T(8,128)} async-done(((f32[32,8192]{1,0:T(8,128)}), f32[32,8192]{1,0:T(8,128)}) %all-reduce.3.cloned.1.call-update) | async-done | bytes 1048592 | tf_op jit(solution)/shard_map/psum | solution.py:103
  498.7 2.3 convolution_add_fusion
  500.9 1.0 fusion.973
  501.9 2.0 fusion.972
  503.9 74.2 %psum.46 = f32[32,32]{1,0:T(8,128)S(1)} all-reduce(f32[32,32]{1,0:T(8,128)S(1)} %fusion.973), channel_id=1, replica_groups=mesh['row'=16,'col'=16] {'row'}, use_global_device_ids=true, to_apply=%region_133.134 | all-reduce | flops 1024 | bytes 8192 | tf_op jit(solution)/shard_map/psum | solution.py:104
  578.5 2.3 fusion
  580.9 69.7 %psum.47 = f32[32,128]{1,0:T(8,128)S(1)} all-reduce(f32[32,128]{1,0:T(8,128)S(1)} %dynamic-slice_select_fusion), channel_id=1, replica_groups=mesh['row'=16,'col'=16] {'row'}, use_global_device_ids=true, to_apply=%region_134.135 | all-reduce | flops 4096 | bytes 32768 | tf_op jit(solution)/shard_map/psum | solution.py:9
  650.6 8.5 %convolution_subtract_fusion.1 = f32[8192,128]{1,0:T(8,128)S(1)} fusion(f32[8192,128]{1,0:T(8,128)} %param.5, f32[32,8192]{1,0:T(8,128)S(1)} %scatter-add.4, f32[32,128]{1,0:T(8,128)S(1)} %psum.47), kind=kOutput, calls=%fused_computation.2 | convolution fusion | flops 403701760 | bytes 9453568 | tf_op jit(solution)/shard_map/dot_general | solution.py:17
  659.2 8.3 %convolution_subtract_fusion = f32[8192,128]{1,0:T(8,128)} fusion(f32[8192,128]{1,0:T(8,128)S(1)} %convolution_subtract_fusion.1, f32[32,8192]{1,0:T(8,128)S(1)} %fusion, f32[32,128]{1,0:T(8,128)S(1)} %psum.44), kind=kOutput, calls=%fused_computation.1 | convolution fusion | flops 403701760 | bytes 9453568 | tf_op jit(solution)/shard_map/dot_general | solution.py:17
  (403 shorter events, 165.3 us)
Async XLA Ops:
  7.2 491.5 %copy-start = (f32[32,8192]{1,0:T(8,128)S(1)}, f32[32,8192]{1,0:T(8,128)}, u32[]{:S(2)}) copy-start(f32[32,8192]{1,0:T(8,128)} %param.7) | copy-start | bytes 3145732
  7.2 491.5 %all-reduce.3.cloned.1.call-start = ((), (), s32[]{:S(2)}) async-start(), calls=%async_computation | async-start | bytes 2097152 | tf_op jit(solution)/shard_map/psum | solution.py:103
  269.7 40.2 %copy-start.1 = (f32[32,8192]{1,0:T(8,128)S(1)}, f32[32,8192]{1,0:T(8,128)}, u32[]{:S(2)}) copy-start(f32[32,8192]{1,0:T(8,128)} %param.6) | copy-start | bytes 3145732
  580.8 78.3 %copy-start.2 = (f32[32,8192]{1,0:T(8,128)}, f32[32,8192]{1,0:T(8,128)S(1)}, u32[]{:S(2)}) copy-start(f32[32,8192]{1,0:T(8,128)S(1)} %fusion) | copy-start | bytes 3145732
Sparse Core Ops, SparseCore 0:
  389.4 109.2 all-reduce.2
where the time goes:
time: 686 us; the launch traced here: 674 us
  blocking collectives  286 us (42%)
  matrix products  141 us (21%)
  waiting for transfers between devices  106 us (15%)
  other arithmetic  66 us (10%)
  between operations  37.7 us (5%)
  local copies, waits for them, and re-layouts  37.1 us (5%)
    psum x3, blocking collectives, from_root(): return lax.psum(block, axis)  212 us
    dot_general x139, matrix products, product(): jnp.dot(left, right, precision=lax.Precision.HIGHEST, preferred_element_t...  117 us
    psum x1, waiting for transfers between devices, local(): images = lax.psum(local_image, 'col') + far_part  106 us
    psum x1, blocking collectives, local(): inner_block = lax.psum(product(reflectors, images.T), 'row')  74.2 us
    reduce_sum x49, other arithmetic, invert_lower(): pivot = jnp.sum(lower_part[index_row] * onehot)  31.5 us
    dot_general x3, matrix products, contract(): lax.dot_general(left, right, (((left_dim,), (right_dim,)), ((), ())), pre...  24.2 us
    mul x32, other arithmetic, decompose(): upper_part = upper_part - factor[:, None] * upper_part[column][None, :]  21 us
    slice x32, local copies, waits for them, and re-layouts, decompose(): upper_part[column, column]  18.6 us
  transfers between devices with their start and end apart: 1, of which 1 were waited for; matrix products, arithmetic and copies ran while one was open for 1% of the time, Pallas kernels for 0%

commit v1 on v0

--- a/solution.py
+++ b/solution.py
@@ -6,7 +6,7 @@
 
 def from_root(block, axis, owner):
     block = jnp.where(lax.axis_index(axis) == owner, block, jnp.zeros_like(block))
-    return lax.psum(block, axis)
+    return lax.all_gather(block, axis).sum(axis=0)
 
 
 def product(left, right):

time: 686 us -> 616 us (0.90)
  the two profiles are of different devices: /device:TPU:0 before, /device:TPU:2 now
where the time goes in v1:
time: 616 us; the launch traced here: 605 us
  blocking collectives  213 us (35%)
  matrix products  141 us (23%)
  waiting for transfers between devices  111 us (18%)
  other arithmetic  66.1 us (11%)
  between operations  37.8 us (6%)
  local copies, waits for them, and re-layouts  36 us (6%)
    dot_general x139, matrix products, product(): jnp.dot(left, right, precision=lax.Precision.HIGHEST, preferred_element_t...  117 us
    psum x1, waiting for transfers between devices, local(): images = lax.psum(local_image, 'col') + far_part  111 us
    all_gather x3, blocking collectives, from_root(): return lax.all_gather(block, axis).sum(axis=0)  75.9 us
    psum x1, blocking collectives, local(): gram_total = lax.psum(gram_part, 'row')  68.5 us
    psum x1, blocking collectives, local(): inner_block = lax.psum(product(reflectors, images.T), 'row')  68.2 us
    reduce_sum x49, other arithmetic, invert_lower(): pivot = jnp.sum(lower_part[index_row] * onehot)  31.5 us
    dot_general x3, matrix products, contract(): lax.dot_general(left, right, (((left_dim,), (right_dim,)), ((), ())), pre...  24.2 us
    mul x32, other arithmetic, decompose(): upper_part = upper_part - factor[:, None] * upper_part[column][None, :]  21 us
  transfers between devices with their start and end apart: 1, of which 1 were waited for; matrix products, arithmetic and copies ran while one was open for 1% of the time, Pallas kernels for 0%

profile of v1, /device:TPU:2, one launch (start us, length us, event | category | flops | bytes accessed | tf_op | source)
XLA Modules:
  0.0 604.6 jit_solution(17532530433387737667)
XLA Ops:
  9.0 2.5 fusion.969
  11.5 68.5 %psum.21 = f32[32,32]{1,0:T(8,128)S(1)} all-reduce(f32[32,32]{1,0:T(8,128)S(1)} %fusion.969), channel_id=1, replica_groups=mesh['row'=16,'col'=16] {'row'}, use_global_device_ids=true, to_apply=%region_0.0 | all-reduce | flops 1024 | bytes 8192 | tf_op jit(solution)/shard_map/psum | solution.py:91
  161.6 0.9 fusion.131
  164.2 0.9 fusion.134
  165.0 0.9 fusion.135
  165.9 0.9 fusion.136
  166.8 0.9 fusion.137
  167.7 0.9 fusion.138
  169.4 0.9 fusion.140
  172.1 0.9 fusion.143
  173.0 0.9 fusion.144
  176.3 0.9 fusion.148
  178.1 0.9 fusion.150
  179.9 0.9 fusion.152
  184.5 27.7 %all-gather = f32[512,32]{1,0:T(8,128)S(1)} all-gather(f32[32,32]{1,0:T(8,128)S(1)} %copy.14), channel_id=2, replica_groups=mesh['row'=16,'col'=16] {'row'}, dimensions={0}, use_global_device_ids=true | all-gather | bytes 69632 | tf_op jit(solution)/shard_map/all_gather | solution.py:9
  214.6 0.9 fusion.160
  273.2 0.9 fusion.195
  275.6 0.9 fusion.197
  277.1 0.9 fusion.198
  278.0 0.9 fusion.199
  280.3 0.9 fusion.201
  282.7 0.9 fusion.203
  284.3 0.9 fusion.204
  287.8 0.9 fusion.165
  289.4 0.9 fusion.167
  290.3 0.9 fusion.168
  291.2 0.9 fusion.169
  292.1 1.0 fusion.170
  293.0 0.9 fusion.171
  294.0 0.9 fusion.172
  296.4 0.9 fusion.206
  298.8 0.9 fusion.208
  301.1 0.9 fusion.175
  302.0 0.9 fusion.176
  304.5 0.9 fusion.178
  308.4 0.9 fusion.210
  309.3 0.9 fusion.211
  310.1 0.9 fusion.212
  312.5 0.9 fusion.182
  316.5 0.9 fusion.214
  317.3 0.9 fusion.215
  318.2 0.9 fusion.216
  320.6 0.9 fusion.186
  322.9 1.0 fusion.188
  324.6 0.9 fusion.218
  325.5 0.9 fusion.219
  326.4 0.9 fusion.220
  328.8 0.9 fusion.190
  331.1 0.9 fusion.192
  332.4 1.0 fusion.970
  334.7 20.7 %all-gather.1 = f32[512,128]{1,0:T(8,128)S(1)} all-gather(f32[32,128]{1,0:T(8,128)S(1)} %dynamic-slice_select_fusion.1), channel_id=3, replica_groups=mesh['row'=16,'col'=16] {'row'}, dimensions={0}, use_global_device_ids=true | all-gather | bytes 278528 | tf_op jit(solution)/shard_map/all_gather | solution.py:9
  355.4 7.4 %fusion.971 = f32[32,8192]{1,0:T(8,128)} fusion(f32[32,128]{1,0:T(8,128)S(1)} %reduce_sum.1308, f32[8192,128]{1,0:T(8,128)} %param.5), kind=kOutput, calls=%fused_computation.1690 | convolution fusion | flops 402653184 | bytes 5259264 | tf_op jit(solution)/shard_map/dot_general | solution.py:17
  363.5 0.9 fusion.222
  364.4 0.9 fusion.223
  365.3 0.9 fusion.224
  366.5 110.5 %all-reduce.2.cloned.1.call-done = f32[32,8192]{1,0:T(8,128)} async-done(((f32[32,8192]{1,0:T(8,128)}), f32[32,8192]{1,0:T(8,128)}) %all-reduce.2.cloned.1.call-update) | async-done | bytes 1048592 | tf_op jit(solution)/shard_map/psum | solution.py:103
  477.0 2.3 convolution_add_fusion
  479.3 1.0 fusion.973
  480.2 2.0 fusion.972
  482.2 68.2 %psum.23 = f32[32,32]{1,0:T(8,128)S(1)} all-reduce(f32[32,32]{1,0:T(8,128)S(1)} %fusion.973), channel_id=1, replica_groups=mesh['row'=16,'col'=16] {'row'}, use_global_device_ids=true, to_apply=%region_133.134 | all-reduce | flops 1024 | bytes 8192 | tf_op jit(solution)/shard_map/psum | solution.py:104
  550.8 2.3 fusion
  553.1 27.5 %all-gather.2 = f32[512,128]{1,0:T(8,128)S(1)} all-gather(f32[32,128]{1,0:T(8,128)S(1)} %dynamic-slice_select_fusion), channel_id=4, replica_groups=mesh['row'=16,'col'=16] {'row'}, dimensions={0}, use_global_device_ids=true | all-gather | bytes 278528 | tf_op jit(solution)/shard_map/all_gather | solution.py:9
  580.7 8.5 %convolution_subtract_fusion.1 = f32[8192,128]{1,0:T(8,128)S(1)} fusion(f32[8192,128]{1,0:T(8,128)} %param.5, f32[32,8192]{1,0:T(8,128)S(1)} %scatter-add.4, f32[32,128]{1,0:T(8,128)S(1)} %reduce_sum.1309), kind=kOutput, calls=%fused_computation.2 | convolution fusion | flops 403701760 | bytes 9453568 | tf_op jit(solution)/shard_map/dot_general | solution.py:17
  589.2 8.3 %convolution_subtract_fusion = f32[8192,128]{1,0:T(8,128)} fusion(f32[8192,128]{1,0:T(8,128)S(1)} %convolution_subtract_fusion.1, f32[32,8192]{1,0:T(8,128)S(1)} %fusion, f32[32,128]{1,0:T(8,128)S(1)} %reduce_sum.1308), kind=kOutput, calls=%fused_computation.1 | convolution fusion | flops 403701760 | bytes 9453568 | tf_op jit(solution)/shard_map/dot_general | solution.py:17
  (409 shorter events, 165.1 us)
Async XLA Ops:
  7.2 469.8 %copy-start = (f32[32,8192]{1,0:T(8,128)S(1)}, f32[32,8192]{1,0:T(8,128)}, u32[]{:S(2)}) copy-start(f32[32,8192]{1,0:T(8,128)} %param.7) | copy-start | bytes 3145732
  7.2 469.8 %all-reduce.2.cloned.1.call-start = ((), (), s32[]{:S(2)}) async-start(), calls=%async_computation | async-start | bytes 2097152 | tf_op jit(solution)/shard_map/psum | solution.py:103
  100.6 83.8 %slice-start = ((f32[32,8192]{1,0:T(8,128)}), f32[32,32]{1,0:T(8,128)S(1)}, s32[]{:S(2)}) async-start(f32[32,8192]{1,0:T(8,128)} %param.6), calls=%async_computation.1 | async-start | bytes 32768 | tf_op jit(solution)/shard_map/slice | solution.py:90
  292.1 40.3 %copy-start.1 = (f32[32,8192]{1,0:T(8,128)S(1)}, f32[32,8192]{1,0:T(8,128)}, u32[]{:S(2)}) copy-start(f32[32,8192]{1,0:T(8,128)} %param.6) | copy-start | bytes 3145732
  553.1 36.1 %copy-start.2 = (f32[32,8192]{1,0:T(8,128)}, f32[32,8192]{1,0:T(8,128)S(1)}, u32[]{:S(2)}) copy-start(f32[32,8192]{1,0:T(8,128)S(1)} %fusion) | copy-start | bytes 3145732
Sparse Core Ops, SparseCore 0:
  362.9 113.9 all-reduce.1
